TPU v7x, 512 devices: a whole 4x4x16 slice. The times are simulated.
512 devices in a mesh: pb: 128 (over z, x, core), vert: 4 (over y).
Axes of the slice: x: 4, y: 4, z: 16, core: 2. Of those that a mesh axis runs over, the one named last changes fastest.
Arguments:
- orbitals: bfloat16 [256, 32, 1024], P('pb', None, 'vert'), may hold values from -6 to 6
- transition: float32 [256, 256], P('pb'), may hold values from -0.9 to 0.9
- trial: float32 [8, 256, 256], P('vert', 'pb'), may hold values from -6 to 6
- screened: bfloat16 [256, 1024, 1024], P('pb', None, 'vert'), may hold values from -0.00030517578 to 0.00030517578
- bare: bfloat16 [1024, 1024], replicated, may hold values from -6.1035156e-05 to 6.1035156e-05
- cheb: float32 [3], replicated, may hold values from 0.5 to 1.5
- pair_k: int32 [384], P('pb'), may hold values from 0 to 255
- pair_slot: int32 [384], P('pb'), may hold values from 0 to 1
- k_order: int32 [256], replicated, may hold values from 0 to 255, each once
Outputs:
- filtered: float32 [8, 256, 256], P('vert', 'pb')
Inputs may be any that keep to these rules, and one draw needn't show every extreme that they name: The pair i lies with the owner of its momentum transfer 2 * (i // 3) + pair_slot[i]. `k_order`: A permutation of the k-points.
All inputs are finite; a program needn't handle non-finite values.
Results may differ from a plain program's by a relative error of at most 0.0075.
Values may be sent and summed in bfloat16 or wider, within the bound.
No kernel may reach another device: no remote copies, remote signals or barrier semaphores. Data moves between devices by JAX's collectives and lax.ppermute only.
A program may use at most 64 MiB of HBM per device.

v0:
```python
import jax
import jax.numpy as jnp
from jax import lax
from jax.sharding import Mesh
from jax.sharding import PartitionSpec as P

NV = 16
PB = ("pb_0", "pb_1", "pb_2")


def laid_out(blocks, dim):
    shape = list(blocks.shape[1:])
    shape[dim] *= blocks.shape[0]
    return jnp.moveaxis(blocks, 0, dim).reshape(shape)


def gather_in_order(shard, axes, turns):
    blocks = shard[None]
    for k in turns:
        blocks = lax.all_gather(blocks, axes[k], axis=0, tiled=True)
    block = [lax.axis_size(axes[k]) for k in reversed(turns)]
    blocks = blocks.reshape(*block, *shard.shape)
    turned = sorted(range(len(turns)), key=lambda place: turns[len(turns) - 1 - place])
    return blocks.transpose(*turned, *range(len(turns), blocks.ndim)).reshape(-1, *shard.shape)


def gather_axes(shard, axes, turns, dim):
    return laid_out(gather_in_order(shard, axes, turns), dim)


def copy_for_each(shard, axis):
    count = lax.axis_size(axis)
    return lax.all_to_all(
        jnp.broadcast_to(shard[None], (count, *shard.shape)), axis, 0, 0, tiled=True
    )


def collect(shard, axis, dim):
    return laid_out(copy_for_each(shard, axis), dim)


def of_everyone(shard, axis):
    return copy_for_each(shard, axis).sum(axis=0)


def gather_axes_2(shard, axes, dim):
    far, near = axes
    blocks = copy_for_each(copy_for_each(shard, far), near)
    return laid_out(blocks.swapaxes(0, 1).reshape(-1, *shard.shape), dim)


def split_up(shard, dim, count):
    before, after = (shard.shape[:dim], shard.shape[dim + 1 :])
    return jnp.moveaxis(shard.reshape(*before, count, -1, *after), dim, 0)


def summed_on_arrival(shard, axis, dim):
    count = lax.axis_size(axis)
    blocks = lax.all_to_all(split_up(shard, dim, count), axis, 0, 0, tiled=True)
    return jnp.sum(blocks, axis=0)


def sum_in_two_steps(shard, axes, dim):
    far, near = axes
    blocks = split_up(shard, dim, lax.axis_size(far))
    nearer = summed_on_arrival(blocks, near, dim + 1)
    arrived = lax.all_to_all(nearer, far, split_axis=0, concat_axis=0, tiled=True)
    return arrived.sum(axis=0)


def by_axis(shard, axes):
    far, near = axes
    nearer = of_everyone(shard, near)
    return of_everyone(nearer, far)


def body(orbitals, transition, trial, screened, bare, cheb, pair_k, pair_slot, k_order):
    kpoint_local = orbitals.shape[0]
    band_all = orbitals.shape[1]
    point_local = orbitals.shape[2]
    pair_count = pair_k.shape[0]
    kpoint_total = k_order.shape[0]
    valence = NV
    conduction = band_all - valence
    pair_width = valence * conduction
    end_count = 2 * pair_count
    hp = lax.Precision.HIGHEST
    position = lax.axis_index(PB)
    momentum = position * kpoint_local + pair_slot
    partner = jnp.mod(pair_k - momentum, kpoint_total)
    pair_ends = jnp.stack([pair_k, partner], axis=1).reshape(-1)
    owner_rows = jnp.arange(kpoint_total, dtype=jnp.int32)
    destination = jnp.sum(
        jnp.where(pair_ends[:, None] == k_order[None, :], owner_rows[None, :], 0), axis=1
    )
    shard_piece = gather_axes(orbitals, PB, (1, 0, 2), 0)
    row_count = shard_piece.shape[0]
    onehot = (destination[:, None] == jnp.arange(row_count, dtype=jnp.int32)[None, :]).astype(
        jnp.bfloat16
    )
    picked = jnp.dot(onehot, shard_piece.reshape(row_count, -1), preferred_element_type=jnp.float32)
    picked = picked.astype(jnp.bfloat16).reshape(end_count, band_all, point_local)
    val_points = collect(picked[:, :valence, :], "vert", 2)
    point_total = val_points.shape[2]
    val_pairs = val_points.reshape(pair_count, 2, valence, point_total)
    cond_pairs = picked[:, valence:, :].reshape(pair_count, 2, conduction, point_local)

    def build_block(pair_index):
        val_both = val_pairs[pair_index].astype(jnp.float32)
        cond_both = cond_pairs[pair_index].astype(jnp.float32)
        left_pair = (
            (val_both[0][:, None, :] * val_both[1][None, :, :])
            .reshape(valence * valence, point_total)
            .astype(jnp.bfloat16)
        )
        right_pair = (
            (cond_both[0][:, None, :] * cond_both[1][None, :, :])
            .reshape(conduction * conduction, point_local)
            .astype(jnp.bfloat16)
        )
        matrix = screened[pair_slot[pair_index]]
        half_product = jnp.dot(left_pair, matrix, preferred_element_type=jnp.float32).astype(
            jnp.bfloat16
        )
        block_part = lax.dot_general(
            half_product, right_pair, (((1,), (1,)), ((), ())), preferred_element_type=jnp.float32
        )
        return (
            block_part.reshape(valence, valence, conduction, conduction)
            .transpose(0, 2, 1, 3)
            .reshape(pair_width, pair_width)
        )

    block_parts = lax.map(build_block, jnp.arange(pair_count, dtype=jnp.int32))
    blocks = of_everyone(block_parts, "vert")
    gathered_own = collect(orbitals, "vert", 2).astype(jnp.float32)
    products = (
        (gathered_own[:, :valence, None, :] * gathered_own[:, None, valence:, :])
        .reshape(kpoint_local, pair_width, point_total)
        .astype(jnp.bfloat16)
    )

    def pick_trial(shard_piece):
        row_count = shard_piece.shape[1]
        onehot = (destination[:, None] == jnp.arange(row_count, dtype=jnp.int32)[None, :]).astype(
            jnp.bfloat16
        )
        return jnp.einsum("er,nrj->nej", onehot, shard_piece, preferred_element_type=jnp.float32)

    def apply_kernel(current):
        fetched = pick_trial(gather_axes_2(current, (("pb_0", "pb_1"), "pb_2"), 1)).astype(
            jnp.bfloat16
        )
        pair_view = fetched.astype(jnp.float32).reshape(fetched.shape[0], pair_count, 2, pair_width)
        toward_first = jnp.einsum("pij,npj->npi", blocks, pair_view[:, :, 1], precision=hp)
        toward_second = jnp.einsum("pij,npi->npj", blocks, pair_view[:, :, 0], precision=hp)
        results = jnp.stack([toward_first, toward_second], axis=2).reshape(
            fetched.shape[0], end_count, pair_width
        )
        onehot = (
            jnp.arange(kpoint_local * lax.axis_size(PB), dtype=jnp.int32)[:, None]
            == destination[None, :]
        ).astype(jnp.float32)
        screened_term = sum_in_two_steps(
            jnp.einsum("re,nej->rnj", onehot, results, precision=hp), (("pb_0", "pb_1"), "pb_2"), 0
        ).transpose(1, 0, 2)
        partial_density = jnp.einsum(
            "nkj,kjm->nm", current, products, preferred_element_type=jnp.float32
        )
        density = by_axis(partial_density, (("pb_0", "pb_1"), "pb_2")).astype(jnp.bfloat16)
        potential = jnp.einsum(
            "nv,mv->nm", density, bare, preferred_element_type=jnp.float32
        ).astype(jnp.bfloat16)
        bare_term = jnp.einsum(
            "kjm,nm->nkj", products, potential, preferred_element_type=jnp.float32
        )
        return transition[None] * current.astype(jnp.float32) + 2.0 * bare_term - screened_term

    first_step = apply_kernel(trial.astype(jnp.bfloat16))
    second_step = 2.0 * apply_kernel(first_step.astype(jnp.bfloat16)) - trial
    return cheb[0] * trial + cheb[1] * first_step + cheb[2] * second_step


def solution(mesh):
    split = Mesh(
        mesh.devices.reshape(16, 4, 2, mesh.shape["vert"]), ("pb_0", "pb_1", "pb_2", "vert")
    )
    in_specs = (
        P(PB, None, "vert"),
        P(PB, None),
        P("vert", PB, None),
        P(PB, None, "vert"),
        P(),
        P(),
        P(PB),
        P(PB),
        P(),
    )
    out_specs = P("vert", PB, None)
    return jax.shard_map(body, mesh=split, in_specs=in_specs, out_specs=out_specs, check_vma=False)
```

profile of v0, /device:TPU:2, one launch (start us, length us, event | category | flops | bytes accessed | tf_op | source)
XLA Modules:
  0.0 449.6 jit_solution(13693576423494758041)
XLA Ops:
  6.6 17.1 %all-gather = bf16[8,32,256]{2,1,0:T(8,128)(2,1)} all-gather(bf16[2,32,256]{2,1,0:T(8,128)(2,1)} %param.11), channel_id=2, replica_groups=mesh['pb_0'=16,'pb_1'=4,'pb_2'=2,'vert'=4] {'pb_1'}, dimensions={0}, use_global_device_ids=true | all-gather | bytes 163840 | tf_op jit(solution)/shard_map/all_gather | solution.py:20
  23.8 72.9 %all-gather.4.cloned.1.call-done = bf16[64,2,32,256]{3,2,1,0:T(8,128)(2,1)} async-done(((bf16[4,2,32,256]{3,2,1,0:T(8,128)(2,1)}), bf16[64,2,32,256]{3,2,1,0:T(8,128)(2,1)}) %all-gather.4.cloned.1.call-update) | async-done | bytes 2097168 | tf_op jit(solution)/shard_map/all_gather | solution.py:20
  97.4 4.3 all-to-all-start
  102.1 5.5 %all-to-all-done = bf16[4,2,32,256]{3,2,1,0:T(8,128)(2,1)S(1)} async-done(((bf16[4,2,32,256]{3,2,1,0:T(8,128)(2,1)}), bf16[4,2,32,256]{3,2,1,0:T(8,128)(2,1)S(1)}, u32[]{:S(2)}, u32[]{:S(2)}) %all-to-all-start) | async-done | bytes 131104 | tf_op jit(solution)/shard_map/all_to_all | solution.py:33
  108.3 11.3 %all-to-all-start.3 = ((bf16[64,2,2,256]{3,2,1,0:T(2,128)(2,1)}), bf16[64,2,2,256]{3,2,1,0:T(2,128)(2,1)S(1)}, u32[]{:S(2)}, u32[]{:S(2)}) async-start(bf16[64,2,2,256]{3,2,1,0:T(2,128)(2,1)} %broadcast_in_dim.50), calls=%async_computation.3 | async-start | bytes 262144 | tf_op jit(solution)/shard_map/all_to_all | solution.py:33
  119.9 2.6 copy.171
  122.5 4.3 copy.205
  128.2 6.5 %all-to-all-done.3 = bf16[64,2,2,256]{3,2,1,0:T(2,128)(2,1)S(1)} async-done(((bf16[64,2,2,256]{3,2,1,0:T(2,128)(2,1)}), bf16[64,2,2,256]{3,2,1,0:T(2,128)(2,1)S(1)}, u32[]{:S(2)}, u32[]{:S(2)}) %all-to-all-start.3) | async-done | bytes 131104 | tf_op jit(solution)/shard_map/all_to_all | solution.py:33
  135.4 3.4 all-to-all-start.5
  139.8 5.3 %all-to-all-done.5 = bf16[4,6,16,256]{3,2,1,0:T(8,128)(2,1)S(1)} async-done(((bf16[4,6,16,256]{3,2,1,0:T(8,128)(2,1)}), bf16[4,6,16,256]{3,2,1,0:T(8,128)(2,1)S(1)}, u32[]{:S(2)}, u32[]{:S(2)}) %all-to-all-start.5) | async-done | bytes 196640 | tf_op jit(solution)/shard_map/all_to_all | solution.py:33
  145.7 3.2 all-to-all-start.1
  150.5 43.2 %while.10 = (s32[]{:T(128)}, f32[3,256,256]{2,1,0:T(8,128)}, s32[3]{0:T(128)}, bf16[3,2,16,1024]{3,2,1,0:T(8,128)(2,1)}, s32[3]{0:T(128)}, /*index=5*/bf16[2,102...) while((s32[]{:T(128)}, f32[3,256,256]{2,1,0:T(8,128)}, ...), condition=%wide.region_4.5_spmd, body=%wide.region_3.4_spmd.sunk | while | flops 168534016 | bytes 3883733 | solution.py:134
  150.5 1.3 dynamic_slice.30
  157.8 1.3 convolution_convert_fusion.7
  159.9 1.8 convolution_bitcast_fusion.10
  161.7 2.4 broadcast_in_dim.69
  164.9 1.3 dynamic_slice.30
  172.2 1.3 convolution_convert_fusion.7
  174.3 1.8 convolution_bitcast_fusion.10
  176.1 2.4 broadcast_in_dim.69
  179.2 1.3 dynamic_slice.30
  186.6 1.3 convolution_convert_fusion.7
  188.6 1.8 convolution_bitcast_fusion.10
  190.4 2.4 broadcast_in_dim.69
  193.8 3.9 all_to_all.75
  197.7 3.1 broadcast_in_dim.55
  200.8 5.0 %all-to-all-start.6 = ((f32[4,3,256,256]{3,2,1,0:T(8,128)}), f32[4,3,256,256]{3,2,1,0:T(8,128)}, u32[]{:S(2)}, u32[]{:S(2)}) async-start(f32[4,3,256,256]{3,2,1,0:T(8,128)} %broadcast_in_dim.55), calls=%async_computation.6 | async-start | bytes 6291456 | tf_op jit(solution)/shard_map/all_to_all | solution.py:33
  208.2 35.7 %all-to-all-done.6 = f32[4,3,256,256]{3,2,1,0:T(8,128)} async-done(((f32[4,3,256,256]{3,2,1,0:T(8,128)}), f32[4,3,256,256]{3,2,1,0:T(8,128)}, u32[]{:S(2)}, u32[]{:S(2)}) %all-to-all-start.6) | async-done | bytes 3145760 | tf_op jit(solution)/shard_map/all_to_all | solution.py:33
  243.8 3.1 reduce_sum.93
  246.9 1.6 convolution_bitcast_fusion.8
  248.5 1.5 convolution_bitcast_fusion.7
  250.6 4.9 %all_to_all.76 = f32[2,64,2,2,256]{4,1,3,2,0:T(8,128)} all-to-all(f32[2,64,2,2,256]{4,1,3,2,0:T(8,128)S(1)} %convolution_bitcast_fusion.2), channel_id=1, replica_groups=mesh['pb_0'=16,'pb_1'=4,'pb_2'=2,'vert'=4] {'pb_2'}, dimensions={0} | all-to-all | bytes 1048576 | tf_op jit(solution)/shard_map/all_to_all | solution.py:59
  256.4 10.3 %all-to-all-start.2 = ((f32[64,2,1024]{2,1,0:T(2,128)}), f32[64,2,1024]{2,1,0:T(2,128)}, u32[]{:S(2)}, u32[]{:S(2)}) async-start(f32[64,2,1024]{2,1,0:T(2,128)} %broadcast_in_dim.46), calls=%async_computation.2 | async-start | bytes 1048576 | tf_op jit(solution)/shard_map/all_to_all | solution.py:33
  268.8 30.9 %all-to-all-done.2 = f32[64,2,1024]{2,1,0:T(2,128)} async-done(((f32[64,2,1024]{2,1,0:T(2,128)}), f32[64,2,1024]{2,1,0:T(2,128)}, u32[]{:S(2)}, u32[]{:S(2)}) %all-to-all-start.2) | async-done | bytes 524320 | tf_op jit(solution)/shard_map/all_to_all | solution.py:33
  299.7 6.0 %all-to-all-start.8 = ((f32[64,2,2,256]{3,2,1,0:T(2,128)}), f32[64,2,2,256]{3,2,1,0:T(2,128)S(1)}, u32[]{:S(2)}, u32[]{:S(2)}) async-start(f32[64,2,2,256]{3,2,1,0:T(2,128)} %copy.176), calls=%async_computation.8 | async-start | bytes 524288 | tf_op jit(solution)/shard_map/all_to_all | solution.py:67
  306.8 19.9 %all-to-all-done.8 = f32[64,2,2,256]{3,2,1,0:T(2,128)S(1)} async-done(((f32[64,2,2,256]{3,2,1,0:T(2,128)}), f32[64,2,2,256]{3,2,1,0:T(2,128)S(1)}, u32[]{:S(2)}, u32[]{:S(2)}) %all-to-all-start.8) | async-done | bytes 262176 | tf_op jit(solution)/shard_map/all_to_all | solution.py:67
  328.6 5.8 %all-to-all-start.11 = ((bf16[64,2,2,256]{3,2,1,0:T(2,128)(2,1)}), bf16[64,2,2,256]{3,2,1,0:T(2,128)(2,1)S(1)}, u32[]{:S(2)}, u32[]{:S(2)}) async-start(bf16[64,2,2,256]{3,2,1,0:T(2,128)(2,1)} %broadcast_in_dim.58), calls=%async_computation.11 | async-start | bytes 262144 | tf_op jit(solution)/shard_map/all_to_all | solution.py:33
  334.6 15.3 %all-to-all-done.11 = bf16[64,2,2,256]{3,2,1,0:T(2,128)(2,1)S(1)} async-done(((bf16[64,2,2,256]{3,2,1,0:T(2,128)(2,1)}), bf16[64,2,2,256]{3,2,1,0:T(2,128)(2,1)S(1)}, u32[]{:S(2)}, u32[]{:S(2)}) %all-to-all-start.11) | async-done | bytes 131104 | tf_op jit(solution)/shard_map/all_to_all | solution.py:33
  350.2 3.9 all_to_all.77
  356.4 1.6 convolution_bitcast_fusion.6
  358.0 1.5 convolution_bitcast_fusion.5
  360.1 4.9 %all_to_all.78 = f32[2,64,2,2,256]{4,1,3,2,0:T(8,128)} all-to-all(f32[2,64,2,2,256]{4,1,3,2,0:T(8,128)S(1)} %convolution_bitcast_fusion.1), channel_id=1, replica_groups=mesh['pb_0'=16,'pb_1'=4,'pb_2'=2,'vert'=4] {'pb_2'}, dimensions={0} | all-to-all | bytes 1048576 | tf_op jit(solution)/shard_map/all_to_all | solution.py:59
  365.6 3.2 all-to-all-start.9
  370.8 5.4 %all-to-all-start.14 = ((f32[64,2,2,256]{3,2,1,0:T(2,128)}), f32[64,2,2,256]{3,2,1,0:T(2,128)S(1)}, u32[]{:S(2)}, u32[]{:S(2)}) async-start(f32[64,2,2,256]{3,2,1,0:T(2,128)} %copy.187), calls=%async_computation.14 | async-start | bytes 524288 | tf_op jit(solution)/shard_map/all_to_all | solution.py:67
  376.3 22.5 %all-to-all-done.14 = f32[64,2,2,256]{3,2,1,0:T(2,128)S(1)} async-done(((f32[64,2,2,256]{3,2,1,0:T(2,128)}), f32[64,2,2,256]{3,2,1,0:T(2,128)S(1)}, u32[]{:S(2)}, u32[]{:S(2)}) %all-to-all-start.14) | async-done | bytes 262176 | tf_op jit(solution)/shard_map/all_to_all | solution.py:67
  399.7 6.2 %all-to-all-start.10 = ((f32[64,2,1024]{2,1,0:T(2,128)}), f32[64,2,1024]{2,1,0:T(2,128)}, u32[]{:S(2)}, u32[]{:S(2)}) async-start(f32[64,2,1024]{2,1,0:T(2,128)} %broadcast_in_dim.57), calls=%async_computation.10 | async-start | bytes 1048576 | tf_op jit(solution)/shard_map/all_to_all | solution.py:33
  406.7 31.5 %all-to-all-done.10 = f32[64,2,1024]{2,1,0:T(2,128)} async-done(((f32[64,2,1024]{2,1,0:T(2,128)}), f32[64,2,1024]{2,1,0:T(2,128)}, u32[]{:S(2)}, u32[]{:S(2)}) %all-to-all-start.10) | async-done | bytes 524320 | tf_op jit(solution)/shard_map/all_to_all | solution.py:33
  439.3 2.8 fusion.16
  (119 shorter events, 36.7 us)
Async XLA Ops:
  6.5 320.4 %copy-start = (bf16[1024,1024]{1,0:T(8,128)(2,1)S(1)}, bf16[1024,1024]{1,0:T(8,128)(2,1)}, u32[]{:S(2)}) copy-start(bf16[1024,1024]{1,0:T(8,128)(2,1)} %param.15) | copy-start | bytes 6291460
  6.5 90.2 %copy-start.2 = (bf16[2,32,256]{2,1,0:T(8,128)(2,1)S(1)}, bf16[2,32,256]{2,1,0:T(8,128)(2,1)}, u32[]{:S(2)}) copy-start(bf16[2,32,256]{2,1,0:T(8,128)(2,1)} %param.11) | copy-start | bytes 98308
  6.5 95.1 %copy-start.11 = (s32[3]{0:T(128)S(1)}, s32[3]{0:T(128)}, u32[]{:S(2)}) copy-start(s32[3]{0:T(128)} %param.17) | copy-start | bytes 40
  6.5 95.1 %copy-start.13 = (s32[3]{0:T(128)S(1)}, s32[3]{0:T(128)}, u32[]{:S(2)}) copy-start(s32[3]{0:T(128)} %param.18) | copy-start | bytes 40
  6.5 95.3 %copy-start.5 = (f32[2,2,256]{2,1,0:T(2,128)S(1)}, f32[2,2,256]{2,1,0:T(2,128)}, u32[]{:S(2)}) copy-start(f32[2,2,256]{2,1,0:T(2,128)} %param.13) | copy-start | bytes 12292
  6.6 95.3 %copy-start.12 = (s32[256]{0:T(256)S(1)}, s32[256]{0:T(256)}, u32[]{:S(2)}) copy-start(s32[256]{0:T(256)} %param.19) | copy-start | bytes 3076
  6.6 90.1 %all-gather.4.cloned.1.call-start = ((), (), s32[]{:S(2)}) async-start(), calls=%async_computation.15 | async-start | bytes 2228224 | tf_op jit(solution)/shard_map/all_gather | solution.py:20
  23.7 96.2 %all-gather.6.cloned.1.call-start = ((), (), s32[]{:S(2)}) async-start(), calls=%async_computation.16 | async-start | bytes 6291456 | tf_op jit(solution)/shard_map/all_gather | solution.py:20
  97.4 10.3 %all-to-all-start = ((bf16[4,2,32,256]{3,2,1,0:T(8,128)(2,1)}), bf16[4,2,32,256]{3,2,1,0:T(8,128)(2,1)S(1)}, u32[]{:S(2)}, u32[]{:S(2)}) async-start(bf16[4,2,32,256]{3,2,1,0:T(8,128)(2,1)} %broadcast_in_dim.44), calls=%async_computation | async-start | bytes 262144 | tf_op jit(solution)/shard_map/all_to_all | solution.py:33
  101.9 36.9 %copy-start.3 = (bf16[2,2,256]{2,0,1:T(2,128)(2,1)}, bf16[2,2,256]{2,0,1:T(2,128)(2,1)S(1)}, u32[]{:S(2)}) copy-start(bf16[2,2,256]{2,0,1:T(2,128)(2,1)S(1)} %copy.214) | copy-start | bytes 6148
  102.1 24.8 %copy-start.7 = (s32[6]{0:T(128)}, s32[6]{0:T(128)S(1)}, u32[]{:S(2)}) copy-start(s32[6]{0:T(128)S(1)} %select_reduce_fusion) | copy-start | bytes 76
  108.3 26.4 %all-to-all-start.3 = ((bf16[64,2,2,256]{3,2,1,0:T(2,128)(2,1)}), bf16[64,2,2,256]{3,2,1,0:T(2,128)(2,1)S(1)}, u32[]{:S(2)}, u32[]{:S(2)}) async-start(bf16[64,2,2,256]{3,2,1,0:T(2,128)(2,1)} %broadcast_in_dim.50), calls=%async_computation.3 | async-start | bytes 262144 | tf_op jit(solution)/shard_map/all_to_all | solution.py:33
  135.4 9.7 %all-to-all-start.5 = ((bf16[4,6,16,256]{3,2,1,0:T(8,128)(2,1)}), bf16[4,6,16,256]{3,2,1,0:T(8,128)(2,1)S(1)}, u32[]{:S(2)}, u32[]{:S(2)}) async-start(bf16[4,6,16,256]{3,2,1,0:T(8,128)(2,1)} %broadcast_in_dim.54), calls=%async_computation.5 | async-start | bytes 393216 | tf_op jit(solution)/shard_map/all_to_all | solution.py:33
  145.7 47.9 %all-to-all-start.1 = ((f32[2,2,1024]{2,1,0:T(2,128)}), f32[2,2,1024]{2,1,0:T(2,128)S(1)}, u32[]{:S(2)}, u32[]{:S(2)}) async-start(f32[2,2,1024]{2,1,0:T(2,128)} %broadcast_in_dim.45), calls=%async_computation.1 | async-start | bytes 32768 | tf_op jit(solution)/shard_map/all_to_all | solution.py:33
  150.5 43.2 %copy-start.1 = (bf16[64,2,2,256]{3,2,0,1:T(2,128)(2,1)S(1)}, bf16[64,2,2,256]{3,2,0,1:T(2,128)(2,1)}, u32[]{:S(2)}) copy-start(bf16[64,2,2,256]{3,2,0,1:T(2,128)(2,1)} %copy.166) | copy-start | bytes 393220
  200.8 6.2 %copy-start.8 = (s32[6]{0:T(128)S(1)}, s32[6]{0:T(128)}, u32[]{:S(2)}) copy-start(s32[6]{0:T(128)} %copy-done.7) | copy-start | bytes 76
  200.8 43.0 %all-to-all-start.6 = ((f32[4,3,256,256]{3,2,1,0:T(8,128)}), f32[4,3,256,256]{3,2,1,0:T(8,128)}, u32[]{:S(2)}, u32[]{:S(2)}) async-start(f32[4,3,256,256]{3,2,1,0:T(8,128)} %broadcast_in_dim.55), calls=%async_computation.6 | async-start | bytes 6291456 | tf_op jit(solution)/shard_map/all_to_all | solution.py:33
  255.5 71.4 %copy-start.4 = (bf16[2,2,256]{2,0,1:T(2,128)(2,1)S(1)}, bf16[2,2,256]{2,0,1:T(2,128)(2,1)}, u32[]{:S(2)}) copy-start(bf16[2,2,256]{2,0,1:T(2,128)(2,1)} %copy-done.3) | copy-start | bytes 6148
  255.5 71.4 %copy-start.9 = (f32[2,256]{1,0:T(2,128)S(1)}, f32[2,256]{1,0:T(2,128)}, u32[]{:S(2)}) copy-start(f32[2,256]{1,0:T(2,128)} %param.12) | copy-start | bytes 6148
  256.4 43.2 %all-to-all-start.2 = ((f32[64,2,1024]{2,1,0:T(2,128)}), f32[64,2,1024]{2,1,0:T(2,128)}, u32[]{:S(2)}, u32[]{:S(2)}) async-start(f32[64,2,1024]{2,1,0:T(2,128)} %broadcast_in_dim.46), calls=%async_computation.2 | async-start | bytes 1048576 | tf_op jit(solution)/shard_map/all_to_all | solution.py:33
  299.7 27.1 %all-to-all-start.8 = ((f32[64,2,2,256]{3,2,1,0:T(2,128)}), f32[64,2,2,256]{3,2,1,0:T(2,128)S(1)}, u32[]{:S(2)}, u32[]{:S(2)}) async-start(f32[64,2,2,256]{3,2,1,0:T(2,128)} %copy.176), calls=%async_computation.8 | async-start | bytes 524288 | tf_op jit(solution)/shard_map/all_to_all | solution.py:67
  328.6 21.3 %all-to-all-start.11 = ((bf16[64,2,2,256]{3,2,1,0:T(2,128)(2,1)}), bf16[64,2,2,256]{3,2,1,0:T(2,128)(2,1)S(1)}, u32[]{:S(2)}, u32[]{:S(2)}) async-start(bf16[64,2,2,256]{3,2,1,0:T(2,128)(2,1)} %broadcast_in_dim.58), calls=%async_computation.11 | async-start | bytes 262144 | tf_op jit(solution)/shard_map/all_to_all | solution.py:33
  360.1 45.8 %copy-start.10 = (f32[3]{0:T(128)S(1)}, f32[3]{0:T(128)}, u32[]{:S(2)}) copy-start(f32[3]{0:T(128)} %param.16) | copy-start | bytes 40
  365.6 5.3 %all-to-all-start.9 = ((f32[2,2,1024]{2,1,0:T(2,128)}), f32[2,2,1024]{2,1,0:T(2,128)S(1)}, u32[]{:S(2)}, u32[]{:S(2)}) async-start(f32[2,2,1024]{2,1,0:T(2,128)} %broadcast_in_dim.56), calls=%async_computation.9 | async-start | bytes 32768 | tf_op jit(solution)/shard_map/all_to_all | solution.py:33
  368.8 70.5 %copy-start.6 = (f32[2,2,256]{2,1,0:T(2,128)S(1)}, f32[2,2,256]{2,1,0:T(2,128)}, u32[]{:S(2)}) copy-start(f32[2,2,256]{2,1,0:T(2,128)} %param.13) | copy-start | bytes 12292
  370.8 27.9 %all-to-all-start.14 = ((f32[64,2,2,256]{3,2,1,0:T(2,128)}), f32[64,2,2,256]{3,2,1,0:T(2,128)S(1)}, u32[]{:S(2)}, u32[]{:S(2)}) async-start(f32[64,2,2,256]{3,2,1,0:T(2,128)} %copy.187), calls=%async_computation.14 | async-start | bytes 524288 | tf_op jit(solution)/shard_map/all_to_all | solution.py:67
  399.7 38.4 %all-to-all-start.10 = ((f32[64,2,1024]{2,1,0:T(2,128)}), f32[64,2,1024]{2,1,0:T(2,128)}, u32[]{:S(2)}, u32[]{:S(2)}) async-start(f32[64,2,1024]{2,1,0:T(2,128)} %broadcast_in_dim.57), calls=%async_computation.10 | async-start | bytes 1048576 | tf_op jit(solution)/shard_map/all_to_all | solution.py:33
Sparse Core Ops, SparseCore 0:
  23.8 72.7 all-gather.3
  98.8 21.0 all-gather.5
where the time goes:
time: 452 us; the launch traced here: 450 us
  waiting for transfers between devices  246 us (54%)
  starting transfers between devices  64 us (14%)
  local copies, waits for them, and re-layouts  42.1 us (9%)
  blocking collectives  34.8 us (8%)
  matrix products  23.8 us (5%)
  between operations  13.8 us (3%)
  other arithmetic  13.4 us (3%)
  loops' own time  11.5 us (3%)
    all_to_all x9, waiting for transfers between devices, copy_for_each(): lax.all_to_all(jnp.broadcast_to(shard[None], (count, *shard.shape)), axis...  131 us
    all_gather x2, waiting for transfers between devices, gather_in_order(): blocks = lax.all_gather(blocks, axes[k], axis=0, tiled=True)  72.9 us
    all_to_all x9, starting transfers between devices, copy_for_each(): lax.all_to_all(jnp.broadcast_to(shard[None], (count, *shard.shape)), axis...  52.6 us
    all_to_all x2, waiting for transfers between devices, sum_in_two_steps(): lax.all_to_all(nearer, far, split_axis=0, concat_axis=0, tiled=True)  42.4 us
    all_gather x1, blocking collectives, gather_in_order(): blocks = lax.all_gather(blocks, axes[k], axis=0, tiled=True)  17.1 us
    another operation x1, loops' own time, body(): block_parts = lax.map(build_block, jnp.arange(pair_count, dtype=jnp.int32))  11.5 us
    all_to_all x2, starting transfers between devices, sum_in_two_steps(): lax.all_to_all(nearer, far, split_axis=0, concat_axis=0, tiled=True)  11.4 us
    all_to_all x2, blocking collectives, summed_on_arrival(): blocks = lax.all_to_all(split_up(shard, dim, count), axis, 0, 0, tiled=True)  9.81 us
  transfers between devices with their start and end apart: 13, of which 10 were waited for; matrix products, arithmetic and copies ran while one was open for 12% of the time, Pallas kernels for 0%

commit v1 on v0

--- a/solution.py
+++ b/solution.py
@@ -17,7 +17,11 @@
 def gather_in_order(shard, axes, turns):
     blocks = shard[None]
     for k in turns:
-        blocks = lax.all_gather(blocks, axes[k], axis=0, tiled=True)
+        inp = axes[k]
+        g_now = lax.all_to_all(
+            jnp.stack(lax.axis_size(inp) * [blocks]), axis_name=inp, split_axis=0, concat_axis=0
+        )
+        blocks = jnp.concatenate(g_now, axis=0)
     block = [lax.axis_size(axes[k]) for k in reversed(turns)]
     blocks = blocks.reshape(*block, *shard.shape)
     turned = sorted(range(len(turns)), key=lambda place: turns[len(turns) - 1 - place])

time: 452 us -> 476 us (1.053)
  between operations: 13.8 us -> 0.45 us
  waiting for transfers between devices: 246 us -> 259 us
  blocking collectives: 34.8 us -> 47 us
  starting transfers between devices: 64 us -> 71.4 us
    all_to_all x0 -> x1, waiting for transfers between devices: none -> 88.8 us  [gather_in_order(): lax.all_to_all(jnp.stack(lax.axis_size(inp) * [blocks]), axis_name=inp, s...]
    all_gather x2 -> x0, waiting for transfers between devices: 72.9 us -> none  [gather_in_order(): blocks = lax.all_gather(blocks, axes[k], axis=0, tiled=True)]
    all_to_all x0 -> x2, blocking collectives: none -> 20.9 us  [gather_in_order(): lax.all_to_all(jnp.stack(lax.axis_size(inp) * [blocks]), axis_name=inp, s...]
    all_gather x1 -> x0, blocking collectives: 17.1 us -> none  [gather_in_order(): blocks = lax.all_gather(blocks, axes[k], axis=0, tiled=True)]
    all_to_all x0 -> x1, starting transfers between devices: none -> 13.6 us  [gather_in_order(): lax.all_to_all(jnp.stack(lax.axis_size(inp) * [blocks]), axis_name=inp, s...]
    all_to_all x2 -> x3, blocking collectives: 7.89 us -> 16.2 us  [copy_for_each(): lax.all_to_all(jnp.broadcast_to(shard[None], (count, *shard.shape)), axis...]
    all_to_all x9 -> x8, starting transfers between devices: 52.6 us -> 46.4 us  [copy_for_each(): lax.all_to_all(jnp.broadcast_to(shard[None], (count, *shard.shape)), axis...]
    another operation x0 -> x3, local copies, waits for them, and re-layouts: none -> 5.18 us  [the longest x1 2.63 us: gather_in_order(): blocks = blocks.reshape(*block, *shard.shape)]
  transfers between devices with their start and end apart: 13 -> 11, of which waited for: 10 -> 9; matrix products, arithmetic and copies ran while one was open for 12% -> 11% of each run, Pallas kernels for 0% -> 0%
where the time goes in v1:
time: 476 us; the launch traced here: 473 us
  waiting for transfers between devices  259 us (54%)
  starting transfers between devices  71.4 us (15%)
  blocking collectives  47 us (10%)
  local copies, waits for them, and re-layouts  44.7 us (9%)
  matrix products  23.7 us (5%)
  other arithmetic  16 us (3%)
  loops' own time  11.5 us (2%)
    all_to_all x8, waiting for transfers between devices, copy_for_each(): lax.all_to_all(jnp.broadcast_to(shard[None], (count, *shard.shape)), axis...  127 us
    all_to_all x1, waiting for transfers between devices, gather_in_order(): lax.all_to_all(jnp.stack(lax.axis_size(inp) * [blocks]), axis_name=inp, s...  88.8 us
    all_to_all x8, starting transfers between devices, copy_for_each(): lax.all_to_all(jnp.broadcast_to(shard[None], (count, *shard.shape)), axis...  46.4 us
    all_to_all x2, waiting for transfers between devices, sum_in_two_steps(): lax.all_to_all(nearer, far, split_axis=0, concat_axis=0, tiled=True)  42.4 us
    all_to_all x2, blocking collectives, gather_in_order(): lax.all_to_all(jnp.stack(lax.axis_size(inp) * [blocks]), axis_name=inp, s...  20.9 us
    all_to_all x3, blocking collectives, copy_for_each(): lax.all_to_all(jnp.broadcast_to(shard[None], (count, *shard.shape)), axis...  16.2 us
    all_to_all x1, starting transfers between devices, gather_in_order(): lax.all_to_all(jnp.stack(lax.axis_size(inp) * [blocks]), axis_name=inp, s...  13.6 us
    another operation x1, loops' own time, body(): block_parts = lax.map(build_block, jnp.arange(pair_count, dtype=jnp.int32))  11.5 us
  transfers between devices with their start and end apart: 11, of which 9 were waited for; matrix products, arithmetic and copies ran while one was open for 11% of the time, Pallas kernels for 0%

profile of v1, /device:TPU:2, one launch (start us, length us, event | category | flops | bytes accessed | tf_op | source)
XLA Modules:
  0.0 473.4 jit_solution(6426322477262596874)
XLA Ops:
  0.9 12.8 %all_to_all.90 = bf16[4,1,2,32,256]{4,3,2,1,0:T(8,128)(2,1)S(1)} all-to-all(bf16[4,1,2,32,256]{4,3,2,1,0:T(8,128)(2,1)S(1)} %stack.39), channel_id=1, replica_groups=mesh['pb_0'=16,'pb_1'=4,'pb_2'=2,'vert'=4] {'pb_1'}, dimensions={0} | all-to-all | bytes 262144 | tf_op jit(solution)/shard_map/all_to_all | solution.py:21
  14.5 8.4 %all_to_all.91 = bf16[4,2,32,256]{3,2,1,0:T(8,128)(2,1)S(1)} all-to-all(bf16[4,2,32,256]{3,2,1,0:T(8,128)(2,1)S(1)} %broadcast_in_dim.42), channel_id=1, replica_groups=mesh['pb_0'=16,'pb_1'=4,'pb_2'=2,'vert'=4] {'vert'}, dimensions={0} | all-to-all | bytes 262144 | tf_op jit(solution)/shard_map/all_to_all | solution.py:37
  22.8 1.6 stack.40
  24.5 13.6 %all-to-all-start.6 = ((bf16[16,4,2,32,256]{4,3,2,1,0:T(8,128)(2,1)}), bf16[16,4,2,32,256]{4,3,2,1,0:T(8,128)(2,1)}, u32[]{:S(2)}, u32[]{:S(2)}) async-start(bf16[16,4,2,32,256]{4,3,2,1,0:T(8,128)(2,1)} %stack.40), calls=%async_computation.6 | async-start | bytes 4194304 | tf_op jit(solution)/shard_map/all_to_all | solution.py:21
  38.9 88.8 %all-to-all-done.6 = bf16[16,4,2,32,256]{4,3,2,1,0:T(8,128)(2,1)} async-done(((bf16[16,4,2,32,256]{4,3,2,1,0:T(8,128)(2,1)}), bf16[16,4,2,32,256]{4,3,2,1,0:T(8,128)(2,1)}, u32[]{:S(2)}, u32[]{:S(2)}) %all-to-all-start.6) | async-done | bytes 2097184 | tf_op jit(solution)/shard_map/all_to_all | solution.py:21
  127.7 2.6 pad_maximum_fusion
  130.3 8.2 %all_to_all.92 = bf16[2,64,2,32,256]{4,3,2,1,0:T(8,128)(2,1)} all-to-all(bf16[2,64,2,32,256]{4,3,2,1,0:T(8,128)(2,1)S(1)} %pad_maximum_fusion), channel_id=1, replica_groups=mesh['pb_0'=16,'pb_1'=4,'pb_2'=2,'vert'=4] {'pb_2'}, dimensions={0} | all-to-all | bytes 8388608 | tf_op jit(solution)/shard_map/all_to_all | solution.py:21
  139.2 13.0 %all-to-all-start.3 = ((bf16[64,2,2,256]{3,2,1,0:T(2,128)(2,1)}), bf16[64,2,2,256]{3,2,1,0:T(2,128)(2,1)S(1)}, u32[]{:S(2)}, u32[]{:S(2)}) async-start(bf16[64,2,2,256]{3,2,1,0:T(2,128)(2,1)} %broadcast_in_dim.48), calls=%async_computation.3 | async-start | bytes 262144 | tf_op jit(solution)/shard_map/all_to_all | solution.py:37
  152.1 2.6 copy.153
  154.8 4.3 copy.187
  160.4 8.6 %all-to-all-done.3 = bf16[64,2,2,256]{3,2,1,0:T(2,128)(2,1)S(1)} async-done(((bf16[64,2,2,256]{3,2,1,0:T(2,128)(2,1)}), bf16[64,2,2,256]{3,2,1,0:T(2,128)(2,1)S(1)}, u32[]{:S(2)}, u32[]{:S(2)}) %all-to-all-start.3) | async-done | bytes 131104 | tf_op jit(solution)/shard_map/all_to_all | solution.py:37
  169.8 3.4 all-to-all-start.8
  174.1 5.3 %all-to-all-done.8 = bf16[4,6,16,256]{3,2,1,0:T(8,128)(2,1)S(1)} async-done(((bf16[4,6,16,256]{3,2,1,0:T(8,128)(2,1)}), bf16[4,6,16,256]{3,2,1,0:T(8,128)(2,1)S(1)}, u32[]{:S(2)}, u32[]{:S(2)}) %all-to-all-start.8) | async-done | bytes 196640 | tf_op jit(solution)/shard_map/all_to_all | solution.py:37
  180.0 3.2 all-to-all-start.1
  184.8 42.9 %while.10 = (s32[]{:T(128)}, f32[3,256,256]{2,1,0:T(8,128)}, s32[3]{0:T(128)}, bf16[3,2,16,1024]{3,2,1,0:T(8,128)(2,1)}, s32[3]{0:T(128)}, /*index=5*/bf16[2,102...) while((s32[]{:T(128)}, f32[3,256,256]{2,1,0:T(8,128)}, ...), condition=%wide.region_4.5_spmd, body=%wide.region_3.4_spmd.sunk | while | flops 168534016 | bytes 3883733 | solution.py:138
  192.1 1.3 convolution_convert_fusion.7
  194.2 1.7 convolution_bitcast_fusion.10
  196.0 2.4 broadcast_in_dim.66
  206.4 1.3 convolution_convert_fusion.7
  208.5 1.7 convolution_bitcast_fusion.10
  210.3 2.4 broadcast_in_dim.66
  220.8 1.3 convolution_convert_fusion.7
  222.8 1.7 convolution_bitcast_fusion.10
  224.6 2.4 broadcast_in_dim.66
  227.9 3.9 all_to_all.93
  231.9 3.1 broadcast_in_dim.52
  234.9 5.0 %all-to-all-start.9 = ((f32[4,3,256,256]{3,2,1,0:T(8,128)}), f32[4,3,256,256]{3,2,1,0:T(8,128)}, u32[]{:S(2)}, u32[]{:S(2)}) async-start(f32[4,3,256,256]{3,2,1,0:T(8,128)} %broadcast_in_dim.52), calls=%async_computation.9 | async-start | bytes 6291456 | tf_op jit(solution)/shard_map/all_to_all | solution.py:37
  242.3 35.7 %all-to-all-done.9 = f32[4,3,256,256]{3,2,1,0:T(8,128)} async-done(((f32[4,3,256,256]{3,2,1,0:T(8,128)}), f32[4,3,256,256]{3,2,1,0:T(8,128)}, u32[]{:S(2)}, u32[]{:S(2)}) %all-to-all-start.9) | async-done | bytes 3145760 | tf_op jit(solution)/shard_map/all_to_all | solution.py:37
  278.0 3.1 reduce_sum.93
  281.0 1.6 convolution_bitcast_fusion.8
  282.6 1.5 convolution_bitcast_fusion.7
  284.7 4.9 %all_to_all.94 = f32[2,64,2,2,256]{4,1,3,2,0:T(8,128)} all-to-all(f32[2,64,2,2,256]{4,1,3,2,0:T(8,128)S(1)} %convolution_bitcast_fusion.2), channel_id=1, replica_groups=mesh['pb_0'=16,'pb_1'=4,'pb_2'=2,'vert'=4] {'pb_2'}, dimensions={0} | all-to-all | bytes 1048576 | tf_op jit(solution)/shard_map/all_to_all | solution.py:63
  290.5 6.6 %all-to-all-start.2 = ((f32[64,2,1024]{2,1,0:T(2,128)}), f32[64,2,1024]{2,1,0:T(2,128)}, u32[]{:S(2)}, u32[]{:S(2)}) async-start(f32[64,2,1024]{2,1,0:T(2,128)} %broadcast_in_dim.44), calls=%async_computation.2 | async-start | bytes 1048576 | tf_op jit(solution)/shard_map/all_to_all | solution.py:37
  299.2 31.0 %all-to-all-done.2 = f32[64,2,1024]{2,1,0:T(2,128)} async-done(((f32[64,2,1024]{2,1,0:T(2,128)}), f32[64,2,1024]{2,1,0:T(2,128)}, u32[]{:S(2)}, u32[]{:S(2)}) %all-to-all-start.2) | async-done | bytes 524320 | tf_op jit(solution)/shard_map/all_to_all | solution.py:37
  330.2 5.9 %all-to-all-start.11 = ((f32[64,2,2,256]{3,2,1,0:T(2,128)}), f32[64,2,2,256]{3,2,1,0:T(2,128)S(1)}, u32[]{:S(2)}, u32[]{:S(2)}) async-start(f32[64,2,2,256]{3,2,1,0:T(2,128)} %copy.158), calls=%async_computation.11 | async-start | bytes 524288 | tf_op jit(solution)/shard_map/all_to_all | solution.py:71
  337.4 20.0 %all-to-all-done.11 = f32[64,2,2,256]{3,2,1,0:T(2,128)S(1)} async-done(((f32[64,2,2,256]{3,2,1,0:T(2,128)}), f32[64,2,2,256]{3,2,1,0:T(2,128)S(1)}, u32[]{:S(2)}, u32[]{:S(2)}) %all-to-all-start.11) | async-done | bytes 262176 | tf_op jit(solution)/shard_map/all_to_all | solution.py:71
  359.2 5.8 %all-to-all-start.14 = ((bf16[64,2,2,256]{3,2,1,0:T(2,128)(2,1)}), bf16[64,2,2,256]{3,2,1,0:T(2,128)(2,1)S(1)}, u32[]{:S(2)}, u32[]{:S(2)}) async-start(bf16[64,2,2,256]{3,2,1,0:T(2,128)(2,1)} %broadcast_in_dim.55), calls=%async_computation.14 | async-start | bytes 262144 | tf_op jit(solution)/shard_map/all_to_all | solution.py:37
  365.2 15.3 %all-to-all-done.14 = bf16[64,2,2,256]{3,2,1,0:T(2,128)(2,1)S(1)} async-done(((bf16[64,2,2,256]{3,2,1,0:T(2,128)(2,1)}), bf16[64,2,2,256]{3,2,1,0:T(2,128)(2,1)S(1)}, u32[]{:S(2)}, u32[]{:S(2)}) %all-to-all-start.14) | async-done | bytes 131104 | tf_op jit(solution)/shard_map/all_to_all | solution.py:37
  380.8 3.9 all_to_all.95
  387.0 1.6 convolution_bitcast_fusion.6
  388.6 1.5 convolution_bitcast_fusion.5
  390.7 4.9 %all_to_all.96 = f32[2,64,2,2,256]{4,1,3,2,0:T(8,128)} all-to-all(f32[2,64,2,2,256]{4,1,3,2,0:T(8,128)S(1)} %convolution_bitcast_fusion.1), channel_id=1, replica_groups=mesh['pb_0'=16,'pb_1'=4,'pb_2'=2,'vert'=4] {'pb_2'}, dimensions={0} | all-to-all | bytes 1048576 | tf_op jit(solution)/shard_map/all_to_all | solution.py:63
  396.2 3.2 all-to-all-start.12
  401.5 5.4 %all-to-all-start.17 = ((f32[64,2,2,256]{3,2,1,0:T(2,128)}), f32[64,2,2,256]{3,2,1,0:T(2,128)S(1)}, u32[]{:S(2)}, u32[]{:S(2)}) async-start(f32[64,2,2,256]{3,2,1,0:T(2,128)} %copy.169), calls=%async_computation.17 | async-start | bytes 524288 | tf_op jit(solution)/shard_map/all_to_all | solution.py:71
  406.9 22.5 %all-to-all-done.17 = f32[64,2,2,256]{3,2,1,0:T(2,128)S(1)} async-done(((f32[64,2,2,256]{3,2,1,0:T(2,128)}), f32[64,2,2,256]{3,2,1,0:T(2,128)S(1)}, u32[]{:S(2)}, u32[]{:S(2)}) %all-to-all-start.17) | async-done | bytes 262176 | tf_op jit(solution)/shard_map/all_to_all | solution.py:71
  430.3 6.2 %all-to-all-start.13 = ((f32[64,2,1024]{2,1,0:T(2,128)}), f32[64,2,1024]{2,1,0:T(2,128)}, u32[]{:S(2)}, u32[]{:S(2)}) async-start(f32[64,2,1024]{2,1,0:T(2,128)} %broadcast_in_dim.54), calls=%async_computation.13 | async-start | bytes 1048576 | tf_op jit(solution)/shard_map/all_to_all | solution.py:37
  437.3 31.4 %all-to-all-done.13 = f32[64,2,1024]{2,1,0:T(2,128)} async-done(((f32[64,2,1024]{2,1,0:T(2,128)}), f32[64,2,1024]{2,1,0:T(2,128)}, u32[]{:S(2)}, u32[]{:S(2)}) %all-to-all-start.13) | async-done | bytes 524320 | tf_op jit(solution)/shard_map/all_to_all | solution.py:37
  470.0 2.8 fusion.16
  (116 shorter events, 41.5 us)
Async XLA Ops:
  0.0 357.5 %copy-start = (bf16[1024,1024]{1,0:T(8,128)(2,1)S(1)}, bf16[1024,1024]{1,0:T(8,128)(2,1)}, u32[]{:S(2)}) copy-start(bf16[1024,1024]{1,0:T(8,128)(2,1)} %param.15) | copy-start | bytes 6291460
  24.5 13.7 %copy-start.10 = (s32[3]{0:T(128)S(1)}, s32[3]{0:T(128)}, u32[]{:S(2)}) copy-start(s32[3]{0:T(128)} %param.17) | copy-start | bytes 40
  24.5 13.7 %copy-start.12 = (s32[3]{0:T(128)S(1)}, s32[3]{0:T(128)}, u32[]{:S(2)}) copy-start(s32[3]{0:T(128)} %param.18) | copy-start | bytes 40
  24.5 13.9 %copy-start.4 = (f32[2,2,256]{2,1,0:T(2,128)S(1)}, f32[2,2,256]{2,1,0:T(2,128)}, u32[]{:S(2)}) copy-start(f32[2,2,256]{2,1,0:T(2,128)} %param.13) | copy-start | bytes 12292
  24.5 13.9 %copy-start.11 = (s32[256]{0:T(256)S(1)}, s32[256]{0:T(256)}, u32[]{:S(2)}) copy-start(s32[256]{0:T(256)} %param.19) | copy-start | bytes 3076
  24.5 103.2 %all-to-all-start.6 = ((bf16[16,4,2,32,256]{4,3,2,1,0:T(8,128)(2,1)}), bf16[16,4,2,32,256]{4,3,2,1,0:T(8,128)(2,1)}, u32[]{:S(2)}, u32[]{:S(2)}) async-start(bf16[16,4,2,32,256]{4,3,2,1,0:T(8,128)(2,1)} %stack.40), calls=%async_computation.6 | async-start | bytes 4194304 | tf_op jit(solution)/shard_map/all_to_all | solution.py:21
  38.4 134.7 %copy-start.2 = (bf16[2,2,256]{2,0,1:T(2,128)(2,1)}, bf16[2,2,256]{2,0,1:T(2,128)(2,1)S(1)}, u32[]{:S(2)}) copy-start(bf16[2,2,256]{2,0,1:T(2,128)(2,1)S(1)} %copy.196) | copy-start | bytes 6148
  38.6 120.5 %copy-start.6 = (s32[6]{0:T(128)}, s32[6]{0:T(128)S(1)}, u32[]{:S(2)}) copy-start(s32[6]{0:T(128)S(1)} %select_reduce_fusion) | copy-start | bytes 76
  139.2 29.9 %all-to-all-start.3 = ((bf16[64,2,2,256]{3,2,1,0:T(2,128)(2,1)}), bf16[64,2,2,256]{3,2,1,0:T(2,128)(2,1)S(1)}, u32[]{:S(2)}, u32[]{:S(2)}) async-start(bf16[64,2,2,256]{3,2,1,0:T(2,128)(2,1)} %broadcast_in_dim.48), calls=%async_computation.3 | async-start | bytes 262144 | tf_op jit(solution)/shard_map/all_to_all | solution.py:37
  169.8 9.7 %all-to-all-start.8 = ((bf16[4,6,16,256]{3,2,1,0:T(8,128)(2,1)}), bf16[4,6,16,256]{3,2,1,0:T(8,128)(2,1)S(1)}, u32[]{:S(2)}, u32[]{:S(2)}) async-start(bf16[4,6,16,256]{3,2,1,0:T(8,128)(2,1)} %broadcast_in_dim.51), calls=%async_computation.8 | async-start | bytes 393216 | tf_op jit(solution)/shard_map/all_to_all | solution.py:37
  180.0 47.7 %all-to-all-start.1 = ((f32[2,2,1024]{2,1,0:T(2,128)}), f32[2,2,1024]{2,1,0:T(2,128)S(1)}, u32[]{:S(2)}, u32[]{:S(2)}) async-start(f32[2,2,1024]{2,1,0:T(2,128)} %broadcast_in_dim.43), calls=%async_computation.1 | async-start | bytes 32768 | tf_op jit(solution)/shard_map/all_to_all | solution.py:37
  184.8 43.0 %copy-start.1 = (bf16[64,2,2,256]{3,2,0,1:T(2,128)(2,1)S(1)}, bf16[64,2,2,256]{3,2,0,1:T(2,128)(2,1)}, u32[]{:S(2)}) copy-start(bf16[64,2,2,256]{3,2,0,1:T(2,128)(2,1)} %copy.148) | copy-start | bytes 393220
  234.9 6.2 %copy-start.7 = (s32[6]{0:T(128)S(1)}, s32[6]{0:T(128)}, u32[]{:S(2)}) copy-start(s32[6]{0:T(128)} %copy-done.6) | copy-start | bytes 76
  234.9 43.0 %all-to-all-start.9 = ((f32[4,3,256,256]{3,2,1,0:T(8,128)}), f32[4,3,256,256]{3,2,1,0:T(8,128)}, u32[]{:S(2)}, u32[]{:S(2)}) async-start(f32[4,3,256,256]{3,2,1,0:T(8,128)} %broadcast_in_dim.52), calls=%async_computation.9 | async-start | bytes 6291456 | tf_op jit(solution)/shard_map/all_to_all | solution.py:37
  289.6 67.9 %copy-start.3 = (bf16[2,2,256]{2,0,1:T(2,128)(2,1)S(1)}, bf16[2,2,256]{2,0,1:T(2,128)(2,1)}, u32[]{:S(2)}) copy-start(bf16[2,2,256]{2,0,1:T(2,128)(2,1)} %copy-done.2) | copy-start | bytes 6148
  289.6 67.9 %copy-start.8 = (f32[2,256]{1,0:T(2,128)S(1)}, f32[2,256]{1,0:T(2,128)}, u32[]{:S(2)}) copy-start(f32[2,256]{1,0:T(2,128)} %param.12) | copy-start | bytes 6148
  290.5 39.7 %all-to-all-start.2 = ((f32[64,2,1024]{2,1,0:T(2,128)}), f32[64,2,1024]{2,1,0:T(2,128)}, u32[]{:S(2)}, u32[]{:S(2)}) async-start(f32[64,2,1024]{2,1,0:T(2,128)} %broadcast_in_dim.44), calls=%async_computation.2 | async-start | bytes 1048576 | tf_op jit(solution)/shard_map/all_to_all | solution.py:37
  330.2 27.1 %all-to-all-start.11 = ((f32[64,2,2,256]{3,2,1,0:T(2,128)}), f32[64,2,2,256]{3,2,1,0:T(2,128)S(1)}, u32[]{:S(2)}, u32[]{:S(2)}) async-start(f32[64,2,2,256]{3,2,1,0:T(2,128)} %copy.158), calls=%async_computation.11 | async-start | bytes 524288 | tf_op jit(solution)/shard_map/all_to_all | solution.py:71
  359.2 21.3 %all-to-all-start.14 = ((bf16[64,2,2,256]{3,2,1,0:T(2,128)(2,1)}), bf16[64,2,2,256]{3,2,1,0:T(2,128)(2,1)S(1)}, u32[]{:S(2)}, u32[]{:S(2)}) async-start(bf16[64,2,2,256]{3,2,1,0:T(2,128)(2,1)} %broadcast_in_dim.55), calls=%async_computation.14 | async-start | bytes 262144 | tf_op jit(solution)/shard_map/all_to_all | solution.py:37
  390.7 45.8 %copy-start.9 = (f32[3]{0:T(128)S(1)}, f32[3]{0:T(128)}, u32[]{:S(2)}) copy-start(f32[3]{0:T(128)} %param.16) | copy-start | bytes 40
  396.2 5.3 %all-to-all-start.12 = ((f32[2,2,1024]{2,1,0:T(2,128)}), f32[2,2,1024]{2,1,0:T(2,128)S(1)}, u32[]{:S(2)}, u32[]{:S(2)}) async-start(f32[2,2,1024]{2,1,0:T(2,128)} %broadcast_in_dim.53), calls=%async_computation.12 | async-start | bytes 32768 | tf_op jit(solution)/shard_map/all_to_all | solution.py:37
  399.4 70.5 %copy-start.5 = (f32[2,2,256]{2,1,0:T(2,128)S(1)}, f32[2,2,256]{2,1,0:T(2,128)}, u32[]{:S(2)}) copy-start(f32[2,2,256]{2,1,0:T(2,128)} %param.13) | copy-start | bytes 12292
  401.5 27.9 %all-to-all-start.17 = ((f32[64,2,2,256]{3,2,1,0:T(2,128)}), f32[64,2,2,256]{3,2,1,0:T(2,128)S(1)}, u32[]{:S(2)}, u32[]{:S(2)}) async-start(f32[64,2,2,256]{3,2,1,0:T(2,128)} %copy.169), calls=%async_computation.17 | async-start | bytes 524288 | tf_op jit(solution)/shard_map/all_to_all | solution.py:71
  430.3 38.4 %all-to-all-start.13 = ((f32[64,2,1024]{2,1,0:T(2,128)}), f32[64,2,1024]{2,1,0:T(2,128)}, u32[]{:S(2)}, u32[]{:S(2)}) async-start(f32[64,2,1024]{2,1,0:T(2,128)} %broadcast_in_dim.54), calls=%async_computation.13 | async-start | bytes 1048576 | tf_op jit(solution)/shard_map/all_to_all | solution.py:37
